TPU v7x, 32 devices: a whole 2x2x4 slice. The times are simulated.
32 devices in a mesh: dp: 2 (over core), ctx: 4 (over z), vocab: 4 (over y, x).
Axes of the slice: x: 2, y: 2, z: 4, core: 2. Of those that a mesh axis runs over, the one named last changes fastest.
Arguments:
- hidden: bfloat16 [512, 4096], P(('dp', 'ctx')), may hold values from -32 to 32
- head_weight: bfloat16 [4096, 9504], P(None, ('ctx', 'vocab')), may hold values from -2 to 2
- targets: int32 [512], P('dp'), may hold values from 0 to 9503
- segment_ids: int32 [512], P('dp'), may hold values from 0 to 31, as said below
- lengths: int32 [32], replicated, may hold values from 8 to 24, as said below
- loss_mask: int32 [512], P('dp'), may hold values 0 or 1
- advantages: float32 [32], replicated, may hold values from -4 to 4
- ref_logprobs: float32 [512], P('dp'), may hold values from -40 to -2
Outputs:
- grad_hidden: bfloat16 [512, 4096], P(('dp', 'ctx', 'vocab'))
- grad_head: bfloat16 [4096, 9504], P(None, ('ctx', 'vocab'))
Inputs may be any that keep to these rules, and one draw needn't show every extreme that they name: `segment_ids`: each sequence's tokens are contiguous; the tokens b * 64 to (b + 1) * 64 - 1 carry ids b * 4 to (b + 1) * 4 - 1, never falling, each id used. lengths[s] is the number of tokens whose segment id is s.
All inputs are finite; a program needn't handle non-finite values. No bound on the sum of `loss_mask` on one device may be relied on, other than what follows from the above.
Results may differ from a plain program's by a relative error of at most 0.012.
Values may be sent and summed in bfloat16 or wider, within the bound.
A program may use at most 128 MiB of HBM per device.

v0:
```python
import jax
import jax.numpy as jnp
from jax import lax
from jax.sharding import PartitionSpec as P

LOSS_SCALE = 1024
kl_weight = 0.1
entropy_weight = 0.05


def per_device(
    hidden, head_weight, targets, segment_ids, lengths, loss_mask, advantages, ref_logprobs
):
    vocab_width = head_weight.shape[1]
    first_column = (
        lax.axis_index("ctx") * lax.axis_size("vocab") + lax.axis_index("vocab")
    ) * vocab_width
    gathered = lax.all_gather(hidden, "ctx", axis=0, tiled=True)
    logits = jnp.dot(gathered, head_weight, preferred_element_type=jnp.float32)
    columns = first_column + lax.iota(jnp.int32, vocab_width)
    target_hits = targets[:, None] == columns[None, :]
    target_part = jnp.sum(jnp.where(target_hits, logits, 0.0), axis=1)
    row_max = lax.pmax(jnp.max(logits, axis=1), ("ctx", "vocab"))
    shifted = jnp.exp(logits - row_max[:, None])
    exp_total, exp_logit, target_logit = lax.psum(
        (jnp.sum(shifted, axis=1), jnp.sum(shifted * logits, axis=1), target_part), ("ctx", "vocab")
    )
    log_total = row_max + jnp.log(exp_total)
    target_logp = target_logit - log_total
    mean_logit = exp_logit / exp_total
    probs = jnp.exp(logits - log_total[:, None])
    seq_onehot = segment_ids[:, None] == lax.iota(jnp.int32, advantages.shape[0])[None, :]
    token_adv = jnp.sum(jnp.where(seq_onehot, advantages[None, :], 0.0), axis=1)
    token_len = jnp.sum(jnp.where(seq_onehot, lengths[None, :].astype(jnp.float32), 0.0), axis=1)
    token_weight = LOSS_SCALE * loss_mask.astype(jnp.float32) / token_len
    logp_grad = -token_adv + kl_weight * (target_logp - ref_logprobs)
    inner = logp_grad[:, None] * (target_hits.astype(jnp.float32) - probs)
    inner = inner + entropy_weight * probs * (logits - mean_logit[:, None])
    grad_logits = (token_weight[:, None] * inner).astype(jnp.bfloat16)
    head_local = lax.dot_general(
        gathered, grad_logits, (((0,), (0,)), ((), ())), preferred_element_type=jnp.float32
    ).astype(jnp.bfloat16)
    grad_head = lax.psum(head_local, "dp").astype(jnp.float32).astype(jnp.bfloat16)
    grad_hidden = lax.psum_scatter(
        lax.dot_general(
            grad_logits, head_weight, (((1,), (1,)), ((), ())), preferred_element_type=jnp.float32
        ),
        ("ctx", "vocab"),
        scatter_dimension=0,
        tiled=True,
    )
    return (grad_hidden.astype(jnp.bfloat16), grad_head)


def solution(mesh):
    return jax.shard_map(
        per_device,
        mesh=mesh,
        in_specs=(
            P(("dp", "ctx"), None),
            P(None, ("ctx", "vocab")),
            P("dp"),
            P("dp"),
            P(),
            P("dp"),
            P(),
            P("dp"),
        ),
        out_specs=(P(("dp", "ctx", "vocab"), None), P(None, ("ctx", "vocab"))),
        check_vma=False,
    )
```

profile of v0, /device:TPU:0, one launch (start us, length us, event | category | flops | bytes accessed | tf_op | source)
XLA Modules:
  0.0 282.1 jit_solution(3857916356808033694)
XLA Ops:
  7.2 0.0 all-gather.2.cloned.1.call-start
  7.2 0.7 all-gather.2.cloned.1.call-update
  7.9 0.0 reduce-scatter.2.cloned.1.call-start
  7.9 0.7 convert_element_type.25
  8.6 0.8 select_reduce_fusion.1
  9.4 0.7 multiply_divide_fusion
  10.1 0.0 copy-start.1
  10.1 0.0 copy-start.2
  10.1 47.9 %all-gather.2.cloned.1.call-done = bf16[256,4096]{1,0:T(8,128)(2,1)} async-done(((bf16[64,4096]{1,0:T(8,128)(2,1)}), bf16[256,4096]{1,0:T(8,128)(2,1)}) %all-gather.2.cloned.1.call-update) | async-done | bytes 2097168 | tf_op jit(solution)/shard_map/all_gather | solution.py:18
  58.0 4.5 %fusion.11 = (f32[256]{0:T(256)S(1)}, f32[256,594]{0,1:T(8,128)S(1)}) fusion(bf16[256,4096]{1,0:T(8,128)(2,1)} %all-gather.2.cloned.1.call-done, bf16[4096,594]{0,1:T(8,128)(2,1)} %param.9), kind=kOutput, calls=%fused_computation.21 | convolution fusion | flops 1245860096 | bytes 7572480 | tf_op jit(solution)/shard_map/dot_general | solution.py:19
  62.5 39.5 %pmax.7 = f32[256]{0:T(256)S(1)} all-reduce(f32[256]{0:T(256)S(1)} %get-tuple-element.13), channel_id=1, replica_groups=mesh['dp'=2,'ctx'=4,'vocab'=4] {'ctx','vocab'}, use_global_device_ids=true, to_apply=%region_5.6 | all-reduce | flops 256 | bytes 2048 | tf_op jit(solution)/shard_map/pmax | solution.py:23
  102.0 0.0 copy-done.1
  102.0 0.2 fusion.7
  102.2 36.6 %all-reduce = (f32[256]{0:T(256)S(1)}, f32[256]{0:T(256)S(1)}, f32[256]{0:T(256)S(1)}) all-reduce(f32[256]{0:T(256)S(1)} %get-tuple-element.3, f32[256]{0:T(256)S(1)} %get-tuple-element.2, f32[256]{0:T(256)S(1)} %get-tuple-element.4), channel_id=1, replica_groups=mesh['dp'=2,'ctx'=4,'vocab'=4] {'ctx','vocab'}, use_global_device_ids=true, to_apply=%region_9.10 | all-reduce | flops 768 | bytes 6144 | tf_op jit(solution)/shard_map/psum | solution.py:25
  138.8 0.0 copy-done.2
  138.8 6.5 %fusion.9 = f32[256,4096]{1,0:T(8,128)} fusion(bf16[4096,594]{0,1:T(8,128)(2,1)} %param.9, f32[256,594]{0,1:T(8,128)S(1)} %get-tuple-element.14, f32[256]{0:T(256)S(1)} %get-tuple-element.12, f32[256]{0:T(256)S(1)} %get-tuple-element.11, f32[256]{0:T(256)S(1)} %get-tuple-element.10, s32[256]{0:T(256)S(1)} %copy-done.1, f32[256]{0:T(256)S(1)} %multiply_divide_fusion, ...), kind=kOutput, calls=%fused_computation.20 | convolution fusion | flops 1247380992 | bytes 9676104 | tf_op jit(solution)/shard_map/dot_general | solution.py:45
  145.3 0.0 copy-start
  145.3 0.0 reduce-scatter.2.cloned.1.call-update
  145.3 0.0 all-reduce.3.cloned.1.call-start
  145.4 1.5 copy-done
  146.9 3.9 %fusion = bf16[4096,594]{0,1:T(8,128)(2,1)} fusion(bf16[256,4096]{1,0:T(8,128)(2,1)S(1)} %copy-done, f32[256,594]{0,1:T(8,128)S(1)} %get-tuple-element.14, f32[256]{0:T(256)S(1)} %get-tuple-element.12, f32[256]{0:T(256)S(1)} %get-tuple-element.11, f32[256]{0:T(256)S(1)} %get-tuple-element.10, s32[256]{0:T(256)S(1)} %copy-done.1, ...), kind=kOutput, calls=%fused_computation.1 | convolution fusion | flops 1249814016 | bytes 7578952 | tf_op jit(solution)/shard_map/dot_general | solution.py:40
  150.7 0.0 all-reduce.3.cloned.1.call-update
  150.8 87.7 %reduce-scatter.2.cloned.1.call-done = f32[16,4096]{1,0:T(8,128)} async-done(((f32[256,4096]{1,0:T(8,128)}), f32[16,4096]{1,0:T(8,128)}) %reduce-scatter.2.cloned.1.call-update) | async-done | bytes 262160 | tf_op jit(solution)/shard_map/reduce_scatter | solution.py:44
  238.5 1.6 convert_element_type.28
  240.1 30.2 %all-reduce.3.cloned.1.call-done = bf16[4096,594]{0,1:T(8,128)(2,1)} async-done(((bf16[4096,594]{0,1:T(8,128)(2,1)}), bf16[4096,594]{0,1:T(8,128)(2,1)}) %all-reduce.3.cloned.1.call-update) | async-done | bytes 4866064 | tf_op jit(solution)/shard_map/psum | solution.py:43
  270.3 5.2 %copy.11 = bf16[4096,594]{0,1:T(8,128)(2,1)} copy(bf16[4096,594]{0,1:T(8,128)(2,1)} %all-reduce.3.cloned.1.call-done) | data formatting | bytes 9732096
  (2 shorter events, 0.0 us)
Async XLA Ops:
  7.2 50.8 %all-gather.2.cloned.1.call-start = ((), (), s32[]{:S(2)}) async-start(), calls=%async_computation.1 | async-start | bytes 2621440 | tf_op jit(solution)/shard_map/all_gather | solution.py:18
  7.9 230.6 %reduce-scatter.2.cloned.1.call-start = ((), (), s32[]{:S(2)}) async-start(), calls=%async_computation.2 | async-start | bytes 4456448 | tf_op jit(solution)/shard_map/reduce_scatter | solution.py:44
  10.1 91.9 %copy-start.1 = (s32[256]{0:T(256)S(1)}, s32[256]{0:T(256)}, u32[]{:S(2)}) copy-start(s32[256]{0:T(256)} %param.10) | copy-start | bytes 3076
  10.1 128.7 %copy-start.2 = (f32[256]{0:T(256)S(1)}, f32[256]{0:T(256)}, u32[]{:S(2)}) copy-start(f32[256]{0:T(256)} %param.15) | copy-start | bytes 3076
  145.3 1.6 copy-start
  145.3 125.0 %all-reduce.3.cloned.1.call-start = ((), (), s32[]{:S(2)}) async-start(), calls=%async_computation.3 | async-start | bytes 9830400 | tf_op jit(solution)/shard_map/psum | solution.py:43
Sparse Core Ops, SparseCore 0:
  9.5 48.3 all-gather.1
  145.4 93.0 reduce-scatter.1
  241.6 28.6 all-reduce.2
where the time goes:
time: 282 us
  waiting for transfers between devices  167 us (59%)
  blocking collectives  76.1 us (27%)
  matrix products  14.9 us (5%)
  between operations  13.8 us (5%)
  local copies, waits for them, and re-layouts  6.77 us (2%)
  other arithmetic  3.95 us (1%)
    reduce_scatter x1, waiting for transfers between devices, per_device(): lax.psum_scatter(lax.dot_general(grad_logits, head_weight, (((1,), (1,)),...  87.7 us
    all_gather x1, waiting for transfers between devices, per_device(): gathered = lax.all_gather(hidden, 'ctx', axis=0, tiled=True)  47.9 us
    pmax x1, blocking collectives, per_device(): row_max = lax.pmax(jnp.max(logits, axis=1), ('ctx', 'vocab'))  39.5 us
    psum x1, blocking collectives, per_device(): lax.psum((jnp.sum(shifted, axis=1), jnp.sum(shifted * logits, axis=1), ta...  36.6 us
    psum x1, waiting for transfers between devices, per_device(): lax.psum(head_local, 'dp').astype(jnp.float32).astype(jnp.bfloat16)  30.2 us
    unnamed x7, local copies, waits for them, and re-layouts  6.77 us
    dot_general x1, matrix products, per_device(): lax.dot_general(grad_logits, head_weight, (((1,), (1,)), ((), ())), prefe...  6.48 us
  transfers between devices with their start and end apart: 3, of which 3 were waited for; matrix products, arithmetic and copies ran while one was open for 3% of the time, Pallas kernels for 0%

commit v1 on v0

--- a/solution.py
+++ b/solution.py
@@ -15,7 +15,8 @@
     first_column = (
         lax.axis_index("ctx") * lax.axis_size("vocab") + lax.axis_index("vocab")
     ) * vocab_width
-    gathered = lax.all_gather(hidden, "ctx", axis=0, tiled=True)
+    copies = jnp.concatenate([hidden] * lax.axis_size("ctx"), axis=0)
+    gathered = lax.all_to_all(copies, "ctx", 0, 0, tiled=True)
     logits = jnp.dot(gathered, head_weight, preferred_element_type=jnp.float32)
     columns = first_column + lax.iota(jnp.int32, vocab_width)
     target_hits = targets[:, None] == columns[None, :]

time: 282 us -> 261 us (0.926)
  waiting for transfers between devices: 167 us -> 137 us
  starting transfers between devices: 0.12 us -> 6.39 us
    all_to_all x0 -> x1, waiting for transfers between devices: none -> 48 us  [per_device(): gathered = lax.all_to_all(copies, 'ctx', 0, 0, tiled=True)]
    all_gather x1 -> x0, waiting for transfers between devices: 47.9 us -> none  [per_device(): gathered = lax.all_gather(hidden, 'ctx', axis=0, tiled=True)]
    psum x1, waiting for transfers between devices: 30.2 us -> 0.01 us  [per_device(): lax.psum(head_local, 'dp').astype(jnp.float32).astype(jnp.bfloat16)]
    all_to_all x0 -> x1, starting transfers between devices: none -> 6.35 us  [per_device(): gathered = lax.all_to_all(copies, 'ctx', 0, 0, tiled=True)]
    concatenate x0 -> x1, other arithmetic: none -> 3.4 us  [per_device(): copies = jnp.concatenate([hidden] * lax.axis_size('ctx'), axis=0)]
    unnamed x7 -> x13, local copies, waits for them, and re-layouts: 6.77 us -> 5.27 us
  transfers between devices with their start and end apart: 3 -> 3, of which waited for: 3 -> 2; matrix products, arithmetic and copies ran while one was open for 3% -> 2% of each run, Pallas kernels for 0% -> 0%
where the time goes in v1:
time: 261 us
  waiting for transfers between devices  137 us (52%)
  blocking collectives  76.5 us (29%)
  between operations  15.6 us (6%)
  matrix products  14.2 us (5%)
  starting transfers between devices  6.39 us (2%)
  other arithmetic  5.34 us (2%)
  local copies, waits for them, and re-layouts  5.27 us (2%)
    reduce_scatter x1, waiting for transfers between devices, per_device(): lax.psum_scatter(lax.dot_general(grad_logits, head_weight, (((1,), (1,)),...  89.3 us
    all_to_all x1, waiting for transfers between devices, per_device(): gathered = lax.all_to_all(copies, 'ctx', 0, 0, tiled=True)  48 us
    pmax x1, blocking collectives, per_device(): row_max = lax.pmax(jnp.max(logits, axis=1), ('ctx', 'vocab'))  39.9 us
    psum x1, blocking collectives, per_device(): lax.psum((jnp.sum(shifted, axis=1), jnp.sum(shifted * logits, axis=1), ta...  36.6 us
    dot_general x1, matrix products, per_device(): lax.dot_general(grad_logits, head_weight, (((1,), (1,)), ((), ())), prefe...  6.47 us
    all_to_all x1, starting transfers between devices, per_device(): gathered = lax.all_to_all(copies, 'ctx', 0, 0, tiled=True)  6.35 us
    unnamed x13, local copies, waits for them, and re-layouts  5.27 us
  transfers between devices with their start and end apart: 3, of which 2 were waited for; matrix products, arithmetic and copies ran while one was open for 2% of the time, Pallas kernels for 0%

profile of v1, /device:TPU:0, one launch (start us, length us, event | category | flops | bytes accessed | tf_op | source)
XLA Modules:
  0.0 260.6 jit_solution(1534828503257485814)
XLA Ops:
  8.0 0.0 copy-start.5
  8.0 0.0 copy-start.3
  8.0 0.0 copy-start.4
  8.0 0.0 copy-start.1
  8.0 3.4 %pad_maximum_fusion = bf16[256,4096]{1,0:T(8,128)(2,1)} fusion(bf16[64,4096]{1,0:T(8,128)(2,1)} %param.8), kind=kLoop, calls=%fused_computation.1 | loop fusion | flops 8388608 | bytes 2621440 | tf_op jit(solution)/shard_map/concatenate | solution.py:18
  11.4 6.3 %all-to-all-start = ((bf16[4,64,4096]{2,1,0:T(8,128)(2,1)}), bf16[4,64,4096]{2,1,0:T(8,128)(2,1)S(1)}, u32[]{:S(2)}, u32[]{:S(2)}) async-start(bf16[4,64,4096]{2,1,0:T(8,128)(2,1)} %bitcast.8), calls=%async_computation | async-start | bytes 4194304 | tf_op jit(solution)/shard_map/all_to_all | solution.py:19
  17.8 0.0 reduce-scatter.2.cloned.1.call-start
  17.8 0.0 copy-done.5
  17.8 0.0 copy-done.3
  17.8 0.0 copy-done.4
  17.8 0.1 select_reduce_fusion.1
  17.9 0.0 copy-done.1
  17.9 48.0 %all-to-all-done = bf16[4,64,4096]{2,1,0:T(8,128)(2,1)S(1)} async-done(((bf16[4,64,4096]{2,1,0:T(8,128)(2,1)}), bf16[4,64,4096]{2,1,0:T(8,128)(2,1)S(1)}, u32[]{:S(2)}, u32[]{:S(2)}) %all-to-all-start) | async-done | bytes 2097184 | tf_op jit(solution)/shard_map/all_to_all | solution.py:19
  66.0 0.0 copy-start
  66.0 0.0 copy-start.2
  66.0 3.9 %fusion.10 = (f32[256]{0:T(256)S(1)}, f32[256,594]{0,1:T(8,128)S(1)}) fusion(bf16[256,4096]{1,0:T(8,128)(2,1)S(1)} %bitcast.6, bf16[4096,594]{0,1:T(8,128)(2,1)} %param.9), kind=kOutput, calls=%fused_computation.21 | convolution fusion | flops 1245860096 | bytes 7572480 | tf_op jit(solution)/shard_map/dot_general | solution.py:20
  69.9 39.9 %pmax.7 = f32[256]{0:T(256)S(1)} all-reduce(f32[256]{0:T(256)S(1)} %get-tuple-element.13), channel_id=1, replica_groups=mesh['dp'=2,'ctx'=4,'vocab'=4] {'ctx','vocab'}, use_global_device_ids=true, to_apply=%region_5.6 | all-reduce | flops 256 | bytes 2048 | tf_op jit(solution)/shard_map/pmax | solution.py:24
  109.8 0.0 copy-done
  109.8 0.2 fusion.6
  110.0 36.6 %all-reduce = (f32[256]{0:T(256)S(1)}, f32[256]{0:T(256)S(1)}, f32[256]{0:T(256)S(1)}) all-reduce(f32[256]{0:T(256)S(1)} %get-tuple-element.3, f32[256]{0:T(256)S(1)} %get-tuple-element.2, f32[256]{0:T(256)S(1)} %get-tuple-element.4), channel_id=1, replica_groups=mesh['dp'=2,'ctx'=4,'vocab'=4] {'ctx','vocab'}, use_global_device_ids=true, to_apply=%region_9.10 | all-reduce | flops 768 | bytes 6144 | tf_op jit(solution)/shard_map/psum | solution.py:26
  146.6 0.0 copy-done.2
  146.6 6.5 %fusion.8 = f32[256,4096]{1,0:T(8,128)} fusion(bf16[4096,594]{0,1:T(8,128)(2,1)} %param.9, f32[256,594]{0,1:T(8,128)S(1)} %get-tuple-element.14, f32[256]{0:T(256)S(1)} %get-tuple-element.12, f32[256]{0:T(256)S(1)} %get-tuple-element.11, f32[256]{0:T(256)S(1)} %get-tuple-element.10, s32[256]{0:T(256)S(1)} %copy-done, f32[256]{0:T(256)S(1)} %multiply_divide_fusion, ...), kind=kOutput, calls=%fused_computation.20 | convolution fusion | flops 1247380992 | bytes 9676104 | tf_op jit(solution)/shard_map/dot_general | solution.py:46
  153.1 0.0 reduce-scatter.2.cloned.1.call-update
  153.1 0.0 all-reduce.3.cloned.1.call-start
  153.2 3.8 %convolution_convert_fusion = bf16[4096,594]{0,1:T(8,128)(2,1)} fusion(bf16[256,4096]{1,0:T(8,128)(2,1)S(1)} %bitcast.7, f32[256,594]{0,1:T(8,128)S(1)} %get-tuple-element.14, f32[256]{0:T(256)S(1)} %get-tuple-element.12, f32[256]{0:T(256)S(1)} %get-tuple-element.11, f32[256]{0:T(256)S(1)} %get-tuple-element.10, s32[256]{0:T(256)S(1)} %copy-done, ...), kind=kOutput, calls=%fused_computation | convolution fusion | flops 1249814016 | bytes 7578952 | tf_op jit(solution)/shard_map/dot_general | solution.py:41
  157.0 0.0 all-reduce.3.cloned.1.call-update
  157.0 89.3 %reduce-scatter.2.cloned.1.call-done = f32[16,4096]{1,0:T(8,128)} async-done(((f32[256,4096]{1,0:T(8,128)}), f32[16,4096]{1,0:T(8,128)}) %reduce-scatter.2.cloned.1.call-update) | async-done | bytes 262160 | tf_op jit(solution)/shard_map/reduce_scatter | solution.py:45
  246.3 1.6 convert_element_type.25
  247.9 0.0 all-reduce.3.cloned.1.call-done
  247.9 5.2 %copy.11 = bf16[4096,594]{0,1:T(8,128)(2,1)} copy(bf16[4096,594]{0,1:T(8,128)(2,1)} %all-reduce.3.cloned.1.call-done) | data formatting | bytes 9732096
  (4 shorter events, 0.0 us)
Async XLA Ops:
  8.0 9.8 %copy-start.5 = (s32[32]{0:T(128)S(1)}, s32[32]{0:T(128)}, u32[]{:S(2)}) copy-start(s32[32]{0:T(128)} %param.12) | copy-start | bytes 388
  8.0 9.8 %copy-start.3 = (s32[256]{0:T(256)S(1)}, s32[256]{0:T(256)}, u32[]{:S(2)}) copy-start(s32[256]{0:T(256)} %param.11) | copy-start | bytes 3076
  8.0 9.8 %copy-start.4 = (f32[32]{0:T(128)S(1)}, f32[32]{0:T(128)}, u32[]{:S(2)}) copy-start(f32[32]{0:T(128)} %param.14) | copy-start | bytes 388
  8.0 9.9 %copy-start.1 = (s32[256]{0:T(256)S(1)}, s32[256]{0:T(256)}, u32[]{:S(2)}) copy-start(s32[256]{0:T(256)} %param.13) | copy-start | bytes 3076
  11.4 54.5 %all-to-all-start = ((bf16[4,64,4096]{2,1,0:T(8,128)(2,1)}), bf16[4,64,4096]{2,1,0:T(8,128)(2,1)S(1)}, u32[]{:S(2)}, u32[]{:S(2)}) async-start(bf16[4,64,4096]{2,1,0:T(8,128)(2,1)} %bitcast.8), calls=%async_computation | async-start | bytes 4194304 | tf_op jit(solution)/shard_map/all_to_all | solution.py:19
  17.8 228.5 %reduce-scatter.2.cloned.1.call-start = ((), (), s32[]{:S(2)}) async-start(), calls=%async_computation.2 | async-start | bytes 4456448 | tf_op jit(solution)/shard_map/reduce_scatter | solution.py:45
  66.0 43.8 %copy-start = (s32[256]{0:T(256)S(1)}, s32[256]{0:T(256)}, u32[]{:S(2)}) copy-start(s32[256]{0:T(256)} %param.10) | copy-start | bytes 3076
  66.0 80.6 %copy-start.2 = (f32[256]{0:T(256)S(1)}, f32[256]{0:T(256)}, u32[]{:S(2)}) copy-start(f32[256]{0:T(256)} %param.15) | copy-start | bytes 3076
  153.1 94.8 %all-reduce.3.cloned.1.call-start = ((), (), s32[]{:S(2)}) async-start(), calls=%async_computation.3 | async-start | bytes 9830400 | tf_op jit(solution)/shard_map/psum | solution.py:44
Sparse Core Ops, SparseCore 0:
  153.2 93.0 reduce-scatter.1
Sparse Core Ops, SparseCore 1:
  157.1 26.3 all-reduce.2
